TPU v7x, 32 devices: a whole 2x2x4 slice. The times are simulated.
32 devices in a mesh: dp: 8 (over y, x, core), tensor: 4 (over z).
Axes of the slice: x: 2, y: 2, z: 4, core: 2. Of those that a mesh axis runs over, the one named last changes fastest.
Arguments:
- inputs: bfloat16 [2048, 1792], P('dp', 'tensor'), may hold values from -6 to 6
- cotangent: bfloat16 [2048, 1792], P('dp', 'tensor'), may hold values from -6 to 6
- documents: int32 [2048], P('dp'), may hold values from -1 to 3, as said below
- gains: bfloat16 [2, 1792], P(None, 'tensor'), may hold values from 0.5 to 1.5
- query_key: bfloat16 [1792, 2, 256], P(None, None, 'tensor'), may hold values from -0.125 to 0.125
- value_gate: bfloat16 [1792, 2, 1792], P(None, None, 'tensor'), may hold values from -0.125 to 0.125
- conv_taps: bfloat16 [4, 1792], P(None, 'tensor'), may hold values from -3 to 3
- output_weight: bfloat16 [1792, 1792], P('tensor'), may hold values from -3 to 3
- gate_up: bfloat16 [1792, 2, 4096], P(None, None, 'tensor'), may hold values from -0.125 to 0.125
- down_weight: bfloat16 [4096, 1792], P('tensor'), may hold values from -0.09375 to 0.09375
- gains_moment: float32 [2, 1792], P(None, 'tensor'), may hold values from -60 to 60
- query_key_moment: float32 [1792, 2, 256], P('dp', None, 'tensor'), may hold values from -60 to 60
- value_gate_moment: float32 [1792, 2, 1792], P('dp', None, 'tensor'), may hold values from -60 to 60
- conv_taps_moment: float32 [4, 1792], P(None, 'tensor'), may hold values from -60 to 60
- output_weight_moment: float32 [1792, 1792], P('tensor', 'dp'), may hold values from -60 to 60
- gate_up_moment: float32 [1792, 2, 4096], P('dp', None, 'tensor'), may hold values from -60 to 60
- down_weight_moment: float32 [4096, 1792], P('tensor', 'dp'), may hold values from -60 to 60
- gains_mean: float32 [2, 1792], P(None, 'tensor'), may hold values from -4 to 4
- probe_lookup_smoothed: float32 [1792, 2, 256], P('dp', None, 'tensor'), may hold values from -0.125 to 0.125
- value_gate_mean: float32 [1792, 2, 1792], P('dp', None, 'tensor'), may hold values from -0.125 to 0.125
- conv_taps_mean: float32 [4, 1792], P(None, 'tensor'), may hold values from -3 to 3
- output_weight_mean: float32 [1792, 1792], P('tensor', 'dp'), may hold values from -3 to 3
- gate_up_mean: float32 [1792, 2, 4096], P('dp', None, 'tensor'), may hold values from -0.125 to 0.125
- down_weight_mean: float32 [4096, 1792], P('tensor', 'dp'), may hold values from -0.09375 to 0.09375
Outputs:
- mixed: bfloat16 [2048, 1792], P('dp', 'tensor')
- input_grad: float32 [2048, 1792], P('dp', 'tensor')
- gains_grad: float32 [2, 1792], P(None, 'tensor')
- query_key_grad: float32 [1792, 2, 256], P('dp', None, 'tensor')
- value_gate_grad: float32 [1792, 2, 1792], P('dp', None, 'tensor')
- conv_taps_grad: float32 [4, 1792], P(None, 'tensor')
- output_weight_grad: float32 [1792, 1792], P('tensor', 'dp')
- gate_up_grad: float32 [1792, 2, 4096], P('dp', None, 'tensor')
- down_weight_grad: float32 [4096, 1792], P('tensor', 'dp')
- gains_change: float32 [2, 1792], P(None, 'tensor')
- query_key_change: float32 [1792, 2, 256], P('dp', None, 'tensor')
- value_gate_change: float32 [1792, 2, 1792], P('dp', None, 'tensor')
- conv_taps_change: float32 [4, 1792], P(None, 'tensor')
- output_weight_change: float32 [1792, 1792], P('tensor', 'dp')
- gate_up_change: float32 [1792, 2, 4096], P('dp', None, 'tensor')
- down_weight_change: float32 [4096, 1792], P('tensor', 'dp')
- gains_momentum: float32 [2, 1792], P(None, 'tensor')
- query_key_momentum: float32 [1792, 2, 256], P('dp', None, 'tensor')
- value_gate_momentum: float32 [1792, 2, 1792], P('dp', None, 'tensor')
- conv_taps_momentum: float32 [4, 1792], P(None, 'tensor')
- output_weight_momentum: float32 [1792, 1792], P('tensor', 'dp')
- gate_up_momentum: float32 [1792, 2, 4096], P('dp', None, 'tensor')
- down_weight_momentum: float32 [4096, 1792], P('tensor', 'dp')
- gains_average: float32 [2, 1792], P(None, 'tensor')
- query_key_average: float32 [1792, 2, 256], P('dp', None, 'tensor')
- value_gate_average: float32 [1792, 2, 1792], P('dp', None, 'tensor')
- conv_taps_average: float32 [4, 1792], P(None, 'tensor')
- output_weight_average: float32 [1792, 1792], P('tensor', 'dp')
- gate_up_average: float32 [1792, 2, 4096], P('dp', None, 'tensor')
- down_weight_average: float32 [4096, 1792], P('tensor', 'dp')
Inputs may be any that keep to these rules, and one draw needn't show every extreme that they name: `documents`: within each aligned block of 256 rows the numbers start at 0 and never fall; a document spans at least 64 and at most 256 rows (the last one before padding may be shorter), and the first block holds a single document; each block ends with at least one and fewer than 64 padding rows marked -1, and has no other -1.
All inputs are finite; a program needn't handle non-finite values.
Results may differ from a plain program's by a relative error of at most 0.013.
Values may be sent and summed in bfloat16 or wider, within the bound.
No kernel may reach another device: no remote copies, remote signals or barrier semaphores. Data moves between devices by JAX's collectives and lax.ppermute only.
A program may use at most 192 MiB of HBM per device.

v0:
```python
import math
import jax
import jax.numpy as jnp
from jax import lax
from jax.sharding import PartitionSpec as P

H = 16
F = 16
KERNEL = 4
BLOCK = 256
epsilon = 1e-06
momentum_decay = 0.9
learning_rate = 0.001
average_rate = 0.1


def silu_slope(argument):
    logistic_output = jax.nn.sigmoid(argument)
    return logistic_output * (1.0 + argument * (1.0 - logistic_output))


def shift_down(source, offset, filler):
    pad_width = [(offset, 0)] + [(0, 0)] * (source.ndim - 1)
    return jnp.pad(source, pad_width, constant_values=filler)[: source.shape[0]]


def shift_up(source, offset, filler):
    pad_width = [(0, offset)] + [(0, 0)] * (source.ndim - 1)
    return jnp.pad(source, pad_width, constant_values=filler)[offset:]


def convolve(values_pre, tap_weights, documents):
    summed = values_pre * tap_weights[0]
    for offset in range(1, KERNEL):
        same_doc = (shift_down(documents, offset, -2) == documents)[:, None]
        summed = summed + jnp.where(
            same_doc, shift_down(values_pre, offset, 0.0) * tap_weights[offset], 0.0
        )
    return summed


def advance(grad, weight, moment, average):
    moment_new = momentum_decay * moment + (1.0 - momentum_decay) * grad
    change = -learning_rate * ((1.0 - momentum_decay) * grad + momentum_decay * moment_new)
    average_new = average + average_rate * (weight.astype(jnp.float32) + change - average)
    return (change, moment_new, average_new)


def local(
    inputs,
    cotangent,
    documents,
    gains,
    query_key,
    value_gate,
    conv_taps,
    output_weight,
    gate_up,
    down_weight,
    gains_moment,
    query_key_moment,
    value_gate_moment,
    conv_taps_moment,
    output_weight_moment,
    gate_up_moment,
    down_weight_moment,
    gains_mean,
    probe_lookup_smoothed,
    value_gate_mean,
    conv_taps_mean,
    output_weight_mean,
    gate_up_mean,
    down_weight_mean,
):
    tokens = inputs.shape[0]
    feature_share = inputs.shape[1]
    groups = lax.axis_size("tensor")
    model_width = feature_share * groups
    local_heads = H // groups
    head_size = model_width // H
    score_factor_scale = 1.0 / math.sqrt(F)
    own_start = lax.axis_index("tensor") * feature_share

    def own_columns(source):
        return lax.dynamic_slice_in_dim(source, own_start, feature_share, source.ndim - 1)

    whole_inputs, whole_gains = (
        lax.all_gather(inputs, "tensor", axis=1, tiled=True),
        lax.all_gather(gains, "tensor", axis=1, tiled=True),
    )
    inputs_wide = whole_inputs.astype(jnp.float32)
    gain_one = whole_gains[0].astype(jnp.float32)
    gain_two = whole_gains[1].astype(jnp.float32)
    root_one = lax.rsqrt(jnp.mean(inputs_wide * inputs_wide, axis=1, keepdims=True) + epsilon)
    unit_one = inputs_wide * root_one
    normed = (unit_one * gain_one).astype(jnp.bfloat16)
    projected = jnp.einsum(
        "td,dsf->tsf", normed, query_key, preferred_element_type=jnp.float32
    ).astype(jnp.bfloat16)
    queries = projected[:, 0].reshape(tokens, local_heads, F)
    keys = projected[:, 1].reshape(tokens, local_heads, F)
    mixing = jnp.einsum("td,dsf->tsf", normed, value_gate, preferred_element_type=jnp.float32)
    values_pre = mixing[:, 0]
    gates = mixing[:, 1]
    tap_weights = conv_taps.astype(jnp.float32)
    mixed_values = (
        convolve(values_pre, tap_weights, documents)
        .astype(jnp.bfloat16)
        .reshape(tokens, local_heads, head_size)
    )
    margin = 2 * BLOCK
    key_pad = jnp.pad(keys, ((margin, 0), (0, 0), (0, 0)))
    value_pad = jnp.pad(mixed_values, ((margin, 0), (0, 0), (0, 0)))
    docs_pad = jnp.pad(documents, (margin, 0), constant_values=-2)
    block_count = tokens // BLOCK

    def window(block_index):
        first = block_index * BLOCK
        row_index = first + jnp.arange(BLOCK, dtype=jnp.int32)
        column_index = first - margin + jnp.arange(3 * BLOCK, dtype=jnp.int32)
        allowed = (documents[:, None] == docs_pad[None, :]) & (
            column_index[None, :] <= row_index[:, None]
        )
        attention_scores = (
            jnp.einsum("cyg,jyg->ycj", queries, key_pad, preferred_element_type=jnp.float32)
            * score_factor_scale
        )
        weights = jnp.where(
            allowed[None], 1.0 + attention_scores + 0.5 * attention_scores * attention_scores, 0.0
        )
        return (queries, key_pad, value_pad, allowed, attention_scores, weights)

    def forward_block(block_index):
        query_matrix_rows, lookup_lines_array, value_rows, allowed, attention_scores, weights = (
            window(block_index)
        )
        totals = jnp.sum(weights, axis=2)
        probs = (weights / totals[:, :, None]).astype(jnp.bfloat16)
        result = jnp.einsum("hqk,khe->qhe", probs, value_rows, preferred_element_type=jnp.float32)
        return (result, totals)

    attended, kept_totals = lax.map(forward_block, jnp.arange(block_count, dtype=jnp.int32))
    attended = attended.reshape(tokens, feature_share)
    gate_silu = jax.nn.silu(gates)
    gated = (attended * gate_silu).astype(jnp.bfloat16)
    branch = lax.psum(jnp.dot(gated, output_weight, preferred_element_type=jnp.float32), "tensor")
    hidden = inputs_wide + branch
    root_two = lax.rsqrt(jnp.mean(hidden * hidden, axis=1, keepdims=True) + epsilon)
    unit_two = hidden * root_two
    normed_two = (unit_two * gain_two).astype(jnp.bfloat16)
    inner = jnp.einsum("td,dsf->tsf", normed_two, gate_up, preferred_element_type=jnp.float32)
    opener_before_squash = inner[:, 0]
    up_pre = inner[:, 1]
    unit_silu = jax.nn.silu(opener_before_squash)
    activation = (unit_silu * up_pre).astype(jnp.bfloat16)
    feed = lax.psum_scatter(
        jnp.dot(activation, down_weight, preferred_element_type=jnp.float32).astype(jnp.bfloat16),
        "tensor",
        scatter_dimension=1,
        tiled=True,
    ).astype(jnp.float32)
    mixed = (own_columns(hidden) + feed).astype(jnp.bfloat16)
    masked = jnp.where(documents[:, None] >= 0, cotangent, jnp.zeros_like(cotangent))
    cot_whole = lax.all_gather(masked, "tensor", axis=1, tiled=True)
    down_local = jnp.einsum("tf,td->fd", activation, cot_whole, preferred_element_type=jnp.float32)
    d_act = jnp.einsum("td,fd->tf", cot_whole, down_weight, preferred_element_type=jnp.float32)
    d_inner = jnp.stack(
        [d_act * up_pre * silu_slope(opener_before_squash), d_act * unit_silu], axis=1
    ).astype(jnp.bfloat16)
    gate_up_local = jnp.einsum(
        "td,tsf->dsf", normed_two, d_inner, preferred_element_type=jnp.float32
    )
    d_normed_two = lax.psum(
        jnp.einsum("tsf,dsf->td", d_inner, gate_up, preferred_element_type=jnp.float32), "tensor"
    )
    scaled_two = d_normed_two * gain_two
    gain_two_grad = jnp.sum(d_normed_two * unit_two, axis=0)
    d_hidden = cot_whole.astype(jnp.float32) + root_two * (
        scaled_two - unit_two * jnp.mean(scaled_two * unit_two, axis=1, keepdims=True)
    )
    d_branch = d_hidden.astype(jnp.bfloat16)
    output_local = jnp.einsum("tc,td->cd", gated, d_branch, preferred_element_type=jnp.float32)
    d_gated = jnp.einsum("td,cd->tc", d_branch, output_weight, preferred_element_type=jnp.float32)
    d_attended = (d_gated * gate_silu).astype(jnp.bfloat16).reshape(tokens, local_heads, head_size)
    d_gates = (d_gated * attended * silu_slope(gates)).astype(jnp.bfloat16)

    def backward_block(carry, block_index):
        key_acc, payload_accumulator = carry
        query_matrix_rows, lookup_lines_array, value_rows, allowed, attention_scores, weights = (
            window(block_index)
        )
        totals = kept_totals[block_index]
        probs = weights / totals[:, :, None]
        first = block_index * BLOCK
        value_part = jnp.einsum(
            "hqk,qhe->khe",
            probs.astype(jnp.bfloat16),
            d_attended,
            preferred_element_type=jnp.float32,
        )
        d_probs = jnp.einsum(
            "qhe,khe->hqk", d_attended, value_rows, preferred_element_type=jnp.float32
        )
        d_weights = (d_probs - jnp.sum(d_probs * probs, axis=2, keepdims=True)) / totals[:, :, None]
        logit_slope_delta = jnp.where(
            allowed[None], d_weights * (1.0 + attention_scores), 0.0
        ).astype(jnp.bfloat16)
        query_part = (
            jnp.einsum(
                "ogw,wox->gox",
                logit_slope_delta,
                lookup_lines_array,
                preferred_element_type=jnp.float32,
            )
            * score_factor_scale
        )
        key_part = (
            jnp.einsum(
                "naj,ano->jno",
                logit_slope_delta,
                query_matrix_rows,
                preferred_element_type=jnp.float32,
            )
            * score_factor_scale
        )
        key_acc = key_acc + key_part
        payload_accumulator = payload_accumulator + value_part
        return ((key_acc, payload_accumulator), query_part)

    start_carry = (
        jnp.zeros((tokens + margin, local_heads, F), jnp.float32),
        jnp.zeros((tokens + margin, local_heads, head_size), jnp.float32),
    )
    (key_acc, payload_accumulator), query_parts = lax.scan(
        backward_block, start_carry, jnp.arange(block_count, dtype=jnp.int32)
    )
    d_queries = query_parts.reshape(tokens, local_heads * F).astype(jnp.bfloat16)
    d_keys = key_acc[margin:].reshape(tokens, local_heads * F).astype(jnp.bfloat16)
    d_mixed = payload_accumulator[margin:].reshape(tokens, feature_share)
    d_values = d_mixed * tap_weights[0]
    tap_rows = [jnp.sum(d_mixed * values_pre, axis=0)]
    for offset in range(1, KERNEL):
        same_doc = (shift_down(documents, offset, -2) == documents)[:, None]
        masked_grad = jnp.where(same_doc, d_mixed, 0.0)
        d_values = d_values + shift_up(masked_grad, offset, 0.0) * tap_weights[offset]
        tap_rows.append(jnp.sum(masked_grad * shift_down(values_pre, offset, 0.0), axis=0))
    conv_local = jnp.stack(tap_rows)
    d_query_key = jnp.stack([d_queries, d_keys], axis=1)
    delta_worth_opener = jnp.stack([d_values.astype(jnp.bfloat16), d_gates], axis=1)
    query_key_local = jnp.einsum(
        "td,tsf->dsf", normed, d_query_key, preferred_element_type=jnp.float32
    )
    value_gate_local = jnp.einsum(
        "td,tsf->dsf", normed, delta_worth_opener, preferred_element_type=jnp.float32
    )
    d_normed_part = jnp.einsum(
        "tsf,dsf->td", d_query_key, query_key, preferred_element_type=jnp.float32
    )
    d_normed_part = d_normed_part + jnp.einsum(
        "tsf,dsf->td", delta_worth_opener, value_gate, preferred_element_type=jnp.float32
    )
    d_normed = lax.psum(d_normed_part, "tensor")
    scaled_one = d_normed * gain_one
    full_grad = d_hidden + root_one * (
        scaled_one - unit_one * jnp.mean(scaled_one * unit_one, axis=1, keepdims=True)
    )
    input_grad = own_columns(full_grad)
    gain_one_grad = own_columns(jnp.sum(d_normed * unit_one, axis=0))
    gains_local = jnp.stack([gain_one_grad, own_columns(gain_two_grad)])
    gains_grad, conv_taps_grad = lax.psum((gains_local, conv_local), "dp")
    query_key_grad, value_gate_grad, gate_up_grad, output_weight_grad, down_weight_grad = (
        lax.psum_scatter(query_key_local, "dp", scatter_dimension=0, tiled=True),
        lax.psum_scatter(value_gate_local, "dp", scatter_dimension=0, tiled=True),
        lax.psum_scatter(gate_up_local, "dp", scatter_dimension=0, tiled=True),
        lax.psum_scatter(output_local, "dp", scatter_dimension=1, tiled=True),
        lax.psum_scatter(down_local, "dp", scatter_dimension=1, tiled=True),
    )
    dp_index = lax.axis_index("dp")
    dp_count = lax.axis_size("dp")

    def own_rows(source, axis_dim):
        length = source.shape[axis_dim] // dp_count
        return lax.dynamic_slice_in_dim(source, dp_index * length, length, axis_dim)

    gains_change, gains_momentum, gains_average = advance(
        gains_grad, gains, gains_moment, gains_mean
    )
    query_key_change, query_key_momentum, query_key_average = advance(
        query_key_grad, own_rows(query_key, 0), query_key_moment, probe_lookup_smoothed
    )
    value_gate_change, value_gate_momentum, value_gate_average = advance(
        value_gate_grad, own_rows(value_gate, 0), value_gate_moment, value_gate_mean
    )
    conv_taps_change, conv_taps_momentum, conv_taps_average = advance(
        conv_taps_grad, conv_taps, conv_taps_moment, conv_taps_mean
    )
    output_weight_change, output_weight_momentum, output_weight_average = advance(
        output_weight_grad, own_rows(output_weight, 1), output_weight_moment, output_weight_mean
    )
    gate_up_change, gate_up_momentum, gate_up_average = advance(
        gate_up_grad, own_rows(gate_up, 0), gate_up_moment, gate_up_mean
    )
    down_weight_change, down_weight_momentum, down_weight_average = advance(
        down_weight_grad, own_rows(down_weight, 1), down_weight_moment, down_weight_mean
    )
    return (
        mixed,
        input_grad,
        gains_grad,
        query_key_grad,
        value_gate_grad,
        conv_taps_grad,
        output_weight_grad,
        gate_up_grad,
        down_weight_grad,
        gains_change,
        query_key_change,
        value_gate_change,
        conv_taps_change,
        output_weight_change,
        gate_up_change,
        down_weight_change,
        gains_momentum,
        query_key_momentum,
        value_gate_momentum,
        conv_taps_momentum,
        output_weight_momentum,
        gate_up_momentum,
        down_weight_momentum,
        gains_average,
        query_key_average,
        value_gate_average,
        conv_taps_average,
        output_weight_average,
        gate_up_average,
        down_weight_average,
    )


def solution(mesh):
    return jax.shard_map(
        local,
        mesh=mesh,
        in_specs=(
            P("dp", "tensor"),
            P("dp", "tensor"),
            P("dp"),
            P(None, "tensor"),
            P(None, None, "tensor"),
            P(None, None, "tensor"),
            P(None, "tensor"),
            P("tensor", None),
            P(None, None, "tensor"),
            P("tensor", None),
            P(None, "tensor"),
            P("dp", None, "tensor"),
            P("dp", None, "tensor"),
            P(None, "tensor"),
            P("tensor", "dp"),
            P("dp", None, "tensor"),
            P("tensor", "dp"),
            P(None, "tensor"),
            P("dp", None, "tensor"),
            P("dp", None, "tensor"),
            P(None, "tensor"),
            P("tensor", "dp"),
            P("dp", None, "tensor"),
            P("tensor", "dp"),
        ),
        out_specs=(
            P("dp", "tensor"),
            P("dp", "tensor"),
            P(None, "tensor"),
            P("dp", None, "tensor"),
            P("dp", None, "tensor"),
            P(None, "tensor"),
            P("tensor", "dp"),
            P("dp", None, "tensor"),
            P("tensor", "dp"),
            P(None, "tensor"),
            P("dp", None, "tensor"),
            P("dp", None, "tensor"),
            P(None, "tensor"),
            P("tensor", "dp"),
            P("dp", None, "tensor"),
            P("tensor", "dp"),
            P(None, "tensor"),
            P("dp", None, "tensor"),
            P("dp", None, "tensor"),
            P(None, "tensor"),
            P("tensor", "dp"),
            P("dp", None, "tensor"),
            P("tensor", "dp"),
            P(None, "tensor"),
            P("dp", None, "tensor"),
            P("dp", None, "tensor"),
            P(None, "tensor"),
            P("tensor", "dp"),
            P("dp", None, "tensor"),
            P("tensor", "dp"),
        ),
        check_vma=False,
    )
```

profile of v0, /device:TPU:0, one launch (start us, length us, event | category | flops | bytes accessed | tf_op | source)
XLA Modules:
  0.0 709.4 jit_solution(10752097913392679788)
XLA Ops:
  7.3 23.5 %all_gather.9 = bf16[256,1792]{0,1:T(8,128)(2,1)} all-gather(bf16[256,448]{0,1:T(8,128)(2,1)} %param.24), channel_id=1, replica_groups=mesh['dp'=8,'tensor'=4] {'tensor'}, dimensions={1}, use_global_device_ids=true | all-gather | bytes 1146880 | tf_op jit(solution)/shard_map/all_gather | solution.py:88
  30.8 2.2 copy.107
  33.0 11.9 %all-gather = bf16[4,448,2]{1,2,0:T(2,128)(2,1)S(1)} all-gather(bf16[1,448,2]{1,2,0:T(2,128)(2,1)S(1)} %bitcast.173), channel_id=1, replica_groups=mesh['dp'=8,'tensor'=4] {'tensor'}, dimensions={0}, use_global_device_ids=true | all-gather | bytes 8960 | tf_op jit(solution)/shard_map/all_gather | solution.py:89
  46.6 2.4 fusion.17
  54.6 1.9 fusion.87
  57.5 29.3 %all_gather.11 = bf16[256,1792]{0,1:T(8,128)(2,1)} all-gather(bf16[256,448]{0,1:T(8,128)(2,1)S(1)} %broadcast_select_fusion), channel_id=1, replica_groups=mesh['dp'=8,'tensor'=4] {'tensor'}, dimensions={1}, use_global_device_ids=true | all-gather | bytes 1146880 | tf_op jit(solution)/shard_map/all_gather | solution.py:164
  86.8 56.6 %all-reduce.17.cloned.1.call-done = f32[256,1792]{1,0:T(8,128)} async-done(((f32[256,1792]{1,0:T(8,128)}), f32[256,1792]{1,0:T(8,128)}) %all-reduce.17.cloned.1.call-update) | async-done | bytes 1835024 | tf_op jit(solution)/shard_map/psum | solution.py:146
  143.4 2.2 multiply_reduce_fusion.5
  145.7 6.3 fusion.53
  152.1 2.3 fusion.30
  155.3 3.8 convolution_bitcast_fusion.3
  159.2 2.2 copy.111
  161.4 4.7 fusion.3
  166.3 69.5 %all-reduce.19.cloned.1.call-done = f32[256,1792]{1,0:T(8,128)} async-done(((f32[256,1792]{1,0:T(8,128)}), f32[256,1792]{1,0:T(8,128)}) %all-reduce.19.cloned.1.call-update) | async-done | bytes 1835024 | tf_op jit(solution)/shard_map/psum | solution.py:173
  235.9 3.3 multiply_reduce_fusion.1
  243.4 2.2 fusion.20
  245.6 10.6 %fusion.11 = bf16[768,4,16]{0,2,1:T(8,128)(2,1)} fusion(bf16[256,4,16]{0,2,1:T(8,128)(2,1)S(1)} %bitcast.162, f32[4,256,768]{2,1,0:T(8,128)} %fusion.20, f32[4,256,768]{2,1,0:T(8,128)} %copy-done.47, f32[4,256]{1,0:T(4,128)S(1)} %get-tuple-element.236, pred[256,768]{1,0:T(8,128)(4,1)} %copy-done.28), kind=kOutput, calls=%fused_computation.33 | convolution fusion | flops 37062400 | bytes 6623232 | tf_op jit(solution)/shard_map/while/body/eval_jaxpr/naj,ano->jno/dot_general | solution.py:218
  256.9 10.2 %fusion.12 = bf16[4,16,256]{2,1,0:T(8,128)(2,1)S(1)} fusion(f32[4,256,768]{2,1,0:T(8,128)} %fusion.20, f32[4,256,768]{2,1,0:T(8,128)} %copy-done.47, f32[4,256]{1,0:T(4,128)S(1)} %get-tuple-element.236, pred[256,768]{1,0:T(8,128)(4,1)} %copy-done.28, bf16[256,4,16]{0,2,1:T(8,128)(2,1)} %bitcast.160), kind=kOutput, calls=%fused_computation.35 | convolution fusion | flops 36996864 | bytes 6557696 | tf_op jit(solution)/shard_map/while/body/eval_jaxpr/ogw,wox->gox/dot_general | solution.py:209
  267.2 2.7 fusion.74
  269.9 4.2 convolution_bitcast_fusion.4
  276.4 1.9 multiply_reduce_fusion.8
  281.2 4.0 convolution_bitcast_fusion
  285.5 5.4 fusion.88
  291.9 5.4 fusion.15
  297.3 9.2 %fusion.27 = f32[1792,2,1024]{2,0,1:T(8,128)} fusion(bf16[256,1,1024]{2,0,1:T(8,128)(2,1)} %copy-done.23, bf16[256,1,1024]{2,0,1:T(8,128)(2,1)} %copy-done.22, f32[256,1792]{1,0:T(8,128)} %copy-done.1, f32[1792]{0:T(1024)S(1)} %get-tuple-element.184, f32[256]{0:T(256)S(1)} %add_rsqrt_fusion), kind=kOutput, calls=%fused_computation.71 | convolution fusion | flops 1882521600 | bytes 17571840 | tf_op jit(solution)/shard_map/td,tsf->dsf/dot_general | solution.py:170
  306.6 8.4 %copy.109 = bf16[1792,2,1024]{2,0,1:T(8,128)(2,1)} copy(bf16[1792,2,1024]{2,1,0:T(2,128)(2,1)} %param.32) | data formatting | bytes 14680064 | tf_op args[8]
  315.9 2.1 copy.146
  318.0 2.2 constant_dynamic-slice_fusion
  320.2 2.0 copy.147
  323.3 2.0 add_convert_fusion
  330.9 58.2 %all-reduce.21.cloned.1.call-done = f32[256,1792]{1,0:T(8,128)} async-done(((f32[256,1792]{1,0:T(8,128)}), f32[256,1792]{1,0:T(8,128)}) %all-reduce.21.cloned.1.call-update) | async-done | bytes 1835024 | tf_op jit(solution)/shard_map/psum | solution.py:262
  389.1 2.4 multiply_reduce_fusion.2
  391.5 2.5 dynamic-slice_add_fusion
  394.0 2.0 copy.125
  396.0 23.6 %all-reduce.12 = (f32[2,448]{1,0:T(2,128)S(1)}, f32[4,448]{1,0:T(4,128)S(1)}) all-reduce(f32[2,448]{1,0:T(2,128)S(1)} %pad_maximum_fusion.8, f32[4,448]{1,0:T(4,128)S(1)} %pad_maximum_fusion.7), channel_id=1, replica_groups=mesh['dp'=8,'tensor'=4] {'dp'}, use_global_device_ids=true, to_apply=%region_12.13 | all-reduce | flops 2688 | bytes 21504 | tf_op jit(solution)/shard_map/psum | solution.py:270
  421.0 19.0 %reduce-scatter.23.cloned.1.call-done = f32[224,448]{1,0:T(8,128)} async-done(((f32[1792,448]{1,0:T(8,128)}), f32[224,448]{1,0:T(8,128)}) %reduce-scatter.23.cloned.1.call-update) | async-done | bytes 401424
  440.0 2.0 copy.143
  442.0 2.7 multiply_add_fusion.5
  444.7 66.3 %reduce-scatter.17.cloned.1.call-done = f32[1024,224]{0,1:T(8,128)} async-done(((f32[1024,1792]{0,1:T(8,128)}), f32[1024,224]{0,1:T(8,128)}) %reduce-scatter.17.cloned.1.call-update) | async-done | bytes 917520 | tf_op jit(solution)/shard_map/reduce_scatter | solution.py:276
  511.0 3.9 multiply_add_fusion.2
  514.8 66.4 %reduce-scatter.13.cloned.1.call-done = f32[224,2,448]{2,0,1:T(8,128)} async-done(((f32[1792,2,448]{2,0,1:T(8,128)}), f32[224,2,448]{2,0,1:T(8,128)}) %reduce-scatter.13.cloned.1.call-update) | async-done | bytes 802832 | tf_op jit(solution)/shard_map/reduce_scatter | solution.py:273
  581.3 2.5 multiply_add_fusion.3
  590.3 96.9 %reduce-scatter.15.cloned.1.call-done = f32[224,2,1024]{2,0,1:T(8,128)} async-done(((f32[1792,2,1024]{2,0,1:T(8,128)}), f32[224,2,1024]{2,0,1:T(8,128)}) %reduce-scatter.15.cloned.1.call-update) | async-done | bytes 1835024 | tf_op jit(solution)/shard_map/reduce_scatter | solution.py:274
  687.2 4.6 multiply_add_fusion
  691.8 2.6 copy.129
  694.4 2.6 copy.131
  697.1 2.6 copy.133
  699.7 2.6 copy.127
  (167 shorter events, 36.2 us)
Async XLA Ops:
  7.2 39.3 %copy-start = (bf16[1792,2,448]{0,2,1:T(8,128)(2,1)S(1)}, bf16[1792,2,448]{0,2,1:T(8,128)(2,1)}, u32[]{:S(2)}) copy-start(bf16[1792,2,448]{0,2,1:T(8,128)(2,1)} %param.29) | copy-start | bytes 9633796
  7.2 25.8 %copy-start.36 = (bf16[2,448]{1,0:T(2,128)(2,1)S(1)}, bf16[2,448]{1,0:T(2,128)(2,1)}, u32[]{:S(2)}) copy-start(bf16[2,448]{1,0:T(2,128)(2,1)} %param.27) | copy-start | bytes 5380
  7.2 136.2 %all-reduce.17.cloned.1.call-start = ((), (), s32[]{:S(2)}) async-start(), calls=%async_computation.6 | async-start | bytes 3670016 | tf_op jit(solution)/shard_map/psum | solution.py:146
  46.5 3.4 copy-start.30
  46.6 3.4 copy-start.32
  46.6 3.5 copy-start.3
  46.6 3.5 copy-start.20
  49.0 4.8 copy-start.17
  49.9 1.9 copy-start.8
  50.0 1.8 copy-start.41
  50.0 1.8 copy-start.42
  50.0 1.8 copy-start.43
  51.8 2.0 copy-start.47
  52.6 2.0 copy-start.11
  56.5 179.4 %all-reduce.19.cloned.1.call-start = ((), (), s32[]{:S(2)}) async-start(), calls=%async_computation.7 | async-start | bytes 3670016 | tf_op jit(solution)/shard_map/psum | solution.py:173
  143.4 11.9 %slice-start = ((s8[7340032]{0:T(1024)(128)(4,1)}), s8[4194304]{0:T(1024)(128)(4,1)S(1)}, s32[]{:S(2)}) async-start(s8[7340032]{0:T(1024)(128)(4,1)} %bitcast.136), calls=%async_computation.15 | async-start | bytes 8388608
  145.6 6.4 copy-start.1
  145.6 6.4 copy-start.4
  145.6 6.4 copy-start.29
  145.7 9.6 %slice-start.1 = ((s8[7340032]{0:T(1024)(128)(4,1)}), s8[3145728]{0:T(1024)(128)(4,1)S(1)}, s32[]{:S(2)}) async-start(s8[7340032]{0:T(1024)(128)(4,1)} %bitcast.136), calls=%async_computation.16 | async-start | bytes 6291456
  159.1 163.1 %reduce-scatter.19.cloned.1.call-start = ((), (), s32[]{:S(2)}) async-start(), calls=%async_computation.12 | async-start | bytes 1146880
  166.1 161.9 %reduce-scatter.21.cloned.1.call-start = ((), (), s32[]{:S(2)}) async-start(), calls=%async_computation.13 | async-start | bytes 1032192
  235.9 3.3 copy-start.2
  235.9 3.3 copy-start.6
  239.2 1.9 copy-start.12
  239.2 1.9 copy-start.18
  239.2 2.0 copy-start.26
  241.3 2.1 copy-start.16
  274.1 115.0 %all-reduce.21.cloned.1.call-start = ((), (), s32[]{:S(2)}) async-start(), calls=%async_computation.8 | async-start | bytes 3670016 | tf_op jit(solution)/shard_map/psum | solution.py:262
  274.1 2.2 copy-start.9
  275.5 2.8 copy-start.19
  281.1 158.9 %reduce-scatter.23.cloned.1.call-start = ((), (), s32[]{:S(2)}) async-start(), calls=%async_computation.14 | async-start | bytes 4128768
  285.3 225.7 %reduce-scatter.17.cloned.1.call-start = ((), (), s32[]{:S(2)}) async-start(), calls=%async_computation.11 | async-start | bytes 8257536 | tf_op jit(solution)/shard_map/reduce_scatter | solution.py:276
  290.9 290.3 %reduce-scatter.13.cloned.1.call-start = ((), (), s32[]{:S(2)}) async-start(), calls=%async_computation.9 | async-start | bytes 8257536 | tf_op jit(solution)/shard_map/reduce_scatter | solution.py:273
  297.3 389.9 %reduce-scatter.15.cloned.1.call-start = ((), (), s32[]{:S(2)}) async-start(), calls=%async_computation.10 | async-start | bytes 16515072 | tf_op jit(solution)/shard_map/reduce_scatter | solution.py:274
  318.0 9.9 %copy-start.38 = (f32[448]{0:T(512)S(1)}, f32[448]{0:T(512)}, u32[]{:S(2)}) copy-start(f32[448]{0:T(512)} %get-tuple-element.181) | copy-start | bytes 5380
  318.0 9.9 %copy-start.39 = (f32[448]{0:T(512)S(1)}, f32[448]{0:T(512)}, u32[]{:S(2)}) copy-start(f32[448]{0:T(512)} %get-tuple-element.182) | copy-start | bytes 5380
  318.0 9.9 %copy-start.40 = (f32[448]{0:T(512)S(1)}, f32[448]{0:T(512)}, u32[]{:S(2)}) copy-start(f32[448]{0:T(512)} %get-tuple-element.183) | copy-start | bytes 5380
  329.0 62.4 %copy-start.24 = (f32[224,128]{0,1:T(8,128)}, f32[224,128]{0,1:T(8,128)S(1)}, u32[]{:S(2)}) copy-start(f32[224,128]{0,1:T(8,128)S(1)} %copy.145) | copy-start | bytes 344068
  391.4 28.3 %copy-start.37 = (bf16[2,448]{1,0:T(2,128)(2,1)S(1)}, bf16[2,448]{1,0:T(2,128)(2,1)}, u32[]{:S(2)}) copy-start(bf16[2,448]{1,0:T(2,128)(2,1)} %param.27) | copy-start | bytes 5380
  391.4 28.3 %copy-start.44 = (f32[2,448]{1,0:T(2,128)S(1)}, f32[2,448]{1,0:T(2,128)}, u32[]{:S(2)}) copy-start(f32[2,448]{1,0:T(2,128)} %param.41) | copy-start | bytes 10756
  391.5 28.3 %copy-start.45 = (f32[2,448]{1,0:T(2,128)S(1)}, f32[2,448]{1,0:T(2,128)}, u32[]{:S(2)}) copy-start(f32[2,448]{1,0:T(2,128)} %param.34) | copy-start | bytes 10756
  391.5 28.9 %copy-start.33 = (f32[4,448]{1,0:T(4,128)S(1)}, f32[4,448]{1,0:T(4,128)}, u32[]{:S(2)}) copy-start(f32[4,448]{1,0:T(4,128)} %param.44) | copy-start | bytes 21508
  391.5 28.9 %copy-start.34 = (f32[4,448]{1,0:T(4,128)S(1)}, f32[4,448]{1,0:T(4,128)}, u32[]{:S(2)}) copy-start(f32[4,448]{1,0:T(4,128)} %param.37) | copy-start | bytes 21508
  419.7 95.1 %copy-start.35 = (f32[4,448]{1,0:T(4,128)}, f32[4,448]{1,0:T(4,128)S(1)}, u32[]{:S(2)}) copy-start(f32[4,448]{1,0:T(4,128)S(1)} %get-tuple-element.187) | copy-start | bytes 21508
  419.7 95.1 %copy-start.46 = (f32[2,448]{1,0:T(2,128)}, f32[2,448]{1,0:T(2,128)S(1)}, u32[]{:S(2)}) copy-start(f32[2,448]{1,0:T(2,128)S(1)} %get-tuple-element.186) | copy-start | bytes 10756
  585.4 3.3 copy-start.10
  697.1 2.6 copy-start.7
  (11 other events, 12.1 us)
Sparse Core Ops, SparseCore 0:
  56.6 86.7 all-reduce.16
  159.3 76.5 all-reduce.18
  238.8 24.2 reduce-scatter.18
  274.2 34.3 reduce-scatter.20
  311.4 77.5 all-reduce.20
  392.4 47.5 reduce-scatter.22
  444.0 66.9 reduce-scatter.16
  514.3 66.8 reduce-scatter.12
  584.8 102.3 reduce-scatter.14
where the time goes:
time: 715 us; the launch traced here: 709 us
  waiting for transfers between devices  433 us (61%)
  blocking collectives  88.4 us (12%)
  matrix products  82.2 us (11%)
  local copies, waits for them, and re-layouts  51.1 us (7%)
  other arithmetic  38.7 us (5%)
  between operations  15 us (2%)
    reduce_scatter x1, waiting for transfers between devices, local(): lax.psum_scatter(gate_up_local, 'dp', scatter_dimension=0, tiled=True)  96.9 us
    psum x1, waiting for transfers between devices, local(): lax.psum(jnp.einsum('tsf,dsf->td', d_inner, gate_up, preferred_element_ty...  69.5 us
    reduce_scatter x1, waiting for transfers between devices, local(): lax.psum_scatter(value_gate_local, 'dp', scatter_dimension=0, tiled=True)  66.4 us
    reduce_scatter x1, waiting for transfers between devices, local(): lax.psum_scatter(down_local, 'dp', scatter_dimension=1, tiled=True)  66.3 us
    psum x1, waiting for transfers between devices, local(): d_normed = lax.psum(d_normed_part, 'tensor')  58.2 us
    psum x1, waiting for transfers between devices, local(): lax.psum(jnp.dot(gated, output_weight, preferred_element_type=jnp.float32...  56.6 us
    unnamed x117, local copies, waits for them, and re-layouts  40.9 us
    all_gather x1, blocking collectives, local(): cot_whole = lax.all_gather(masked, 'tensor', axis=1, tiled=True)  29.3 us
  transfers between devices with their start and end apart: 9, of which 7 were waited for; matrix products, arithmetic and copies ran while one was open for 18% of the time, Pallas kernels for 0%

commit v1 on v0

--- a/solution.py
+++ b/solution.py
@@ -170,8 +170,12 @@
     gate_up_local = jnp.einsum(
         "td,tsf->dsf", normed_two, d_inner, preferred_element_type=jnp.float32
     )
-    d_normed_two = lax.psum(
-        jnp.einsum("tsf,dsf->td", d_inner, gate_up, preferred_element_type=jnp.float32), "tensor"
+    d_normed_two = jnp.sum(
+        lax.all_gather(
+            jnp.einsum("tsf,dsf->td", d_inner, gate_up, preferred_element_type=jnp.float32),
+            "tensor",
+        ),
+        axis=0,
     )
     scaled_two = d_normed_two * gain_two
     gain_two_grad = jnp.sum(d_normed_two * unit_two, axis=0)

time: 715 us -> 762 us (1.066)
  waiting for transfers between devices: 433 us -> 475 us
    all_gather x0 -> x1, waiting for transfers between devices: none -> 118 us  [local(): lax.all_gather(jnp.einsum('tsf,dsf->td', d_inner, gate_up, preferred_elem...]
    psum x1 -> x0, waiting for transfers between devices: 69.5 us -> none  [local(): lax.psum(jnp.einsum('tsf,dsf->td', d_inner, gate_up, preferred_element_ty...]
    reduce_scatter x1, waiting for transfers between devices: 66.3 us -> 8.04 us  [local(): lax.psum_scatter(down_local, 'dp', scatter_dimension=1, tiled=True)]
    unnamed x12, waiting for transfers between devices: 19.2 us -> 51.5 us
    psum x1, waiting for transfers between devices: 58.2 us -> 76.9 us  [local(): d_normed = lax.psum(d_normed_part, 'tensor')]
    unnamed x117 -> x115, local copies, waits for them, and re-layouts: 40.9 us -> 41.4 us
  transfers between devices with their start and end apart: 9 -> 9, of which waited for: 7 -> 8; matrix products, arithmetic and copies ran while one was open for 18% -> 17% of each run, Pallas kernels for 0% -> 0%
where the time goes in v1:
time: 762 us; the launch traced here: 756 us
  waiting for transfers between devices  475 us (62%)
  blocking collectives  87.3 us (11%)
  matrix products  83.8 us (11%)
  local copies, waits for them, and re-layouts  51.6 us (7%)
  other arithmetic  43 us (6%)
  between operations  14.7 us (2%)
    all_gather x1, waiting for transfers between devices, local(): lax.all_gather(jnp.einsum('tsf,dsf->td', d_inner, gate_up, preferred_elem...  118 us
    reduce_scatter x1, waiting for transfers between devices, local(): lax.psum_scatter(gate_up_local, 'dp', scatter_dimension=0, tiled=True)  96.9 us
    psum x1, waiting for transfers between devices, local(): d_normed = lax.psum(d_normed_part, 'tensor')  76.9 us
    reduce_scatter x1, waiting for transfers between devices, local(): lax.psum_scatter(value_gate_local, 'dp', scatter_dimension=0, tiled=True)  65.7 us
    psum x1, waiting for transfers between devices, local(): lax.psum(jnp.dot(gated, output_weight, preferred_element_type=jnp.float32...  57.1 us
    unnamed x12, waiting for transfers between devices  51.5 us
    unnamed x115, local copies, waits for them, and re-layouts  41.4 us
    all_gather x1, blocking collectives, local(): cot_whole = lax.all_gather(masked, 'tensor', axis=1, tiled=True)  28.4 us
  transfers between devices with their start and end apart: 9, of which 8 were waited for; matrix products, arithmetic and copies ran while one was open for 17% of the time, Pallas kernels for 0%

profile of v1, /device:TPU:0, one launch (start us, length us, event | category | flops | bytes accessed | tf_op | source)
XLA Modules:
  0.0 756.1 jit_solution(7103852405914927571)
XLA Ops:
  8.3 23.4 %all_gather.15 = bf16[256,1792]{0,1:T(8,128)(2,1)} all-gather(bf16[256,448]{0,1:T(8,128)(2,1)} %param.24), channel_id=1, replica_groups=mesh['dp'=8,'tensor'=4] {'tensor'}, dimensions={1}, use_global_device_ids=true | all-gather | bytes 1146880 | tf_op jit(solution)/shard_map/all_gather | solution.py:88
  31.7 2.2 copy.107
  33.9 11.9 %all-gather.1 = bf16[4,448,2]{1,2,0:T(2,128)(2,1)S(1)} all-gather(bf16[1,448,2]{1,2,0:T(2,128)(2,1)S(1)} %bitcast.175), channel_id=1, replica_groups=mesh['dp'=8,'tensor'=4] {'tensor'}, dimensions={0}, use_global_device_ids=true | all-gather | bytes 8960 | tf_op jit(solution)/shard_map/all_gather | solution.py:89
  47.4 2.4 fusion.17
  58.3 28.4 %all_gather.17 = bf16[256,1792]{0,1:T(8,128)(2,1)} all-gather(bf16[256,448]{0,1:T(8,128)(2,1)S(1)} %broadcast_select_fusion), channel_id=1, replica_groups=mesh['dp'=8,'tensor'=4] {'tensor'}, dimensions={1}, use_global_device_ids=true | all-gather | bytes 1146880 | tf_op jit(solution)/shard_map/all_gather | solution.py:164
  86.7 57.1 %all-reduce.16.cloned.1.call-done = f32[256,1792]{1,0:T(8,128)} async-done(((f32[256,1792]{1,0:T(8,128)}), f32[256,1792]{1,0:T(8,128)}) %all-reduce.16.cloned.1.call-update) | async-done | bytes 1835024 | tf_op jit(solution)/shard_map/psum | solution.py:146
  143.8 2.2 multiply_reduce_fusion.5
  146.1 6.3 fusion.53
  152.5 2.3 fusion.30
  155.7 3.8 convolution_bitcast_fusion.3
  159.6 4.7 fusion.3
  164.4 5.8 fusion.88
  170.5 2.3 copy.111
  172.7 118.5 %all-gather.4.cloned.1.call-done = f32[1024,1792]{1,0:T(8,128)} async-done(((f32[256,1792]{1,0:T(8,128)}), f32[1024,1792]{1,0:T(8,128)}) %all-gather.4.cloned.1.call-update) | async-done | bytes 7340048 | tf_op jit(solution)/shard_map/all_gather | solution.py:174
  291.2 5.0 reduce_sum.122
  296.2 3.3 multiply_reduce_fusion.1
  303.7 2.3 fusion.20
  306.0 10.6 %fusion.11 = bf16[768,4,16]{0,2,1:T(8,128)(2,1)} fusion(bf16[256,4,16]{0,2,1:T(8,128)(2,1)S(1)} %bitcast.164, f32[4,256,768]{2,1,0:T(8,128)} %fusion.20, f32[4,256,768]{2,1,0:T(8,128)} %copy-done.46, f32[4,256]{1,0:T(4,128)S(1)} %get-tuple-element.236, pred[256,768]{1,0:T(8,128)(4,1)} %copy-done.27), kind=kOutput, calls=%fused_computation.33 | convolution fusion | flops 37062400 | bytes 6623232 | tf_op jit(solution)/shard_map/while/body/eval_jaxpr/naj,ano->jno/dot_general | solution.py:222
  317.4 10.2 %fusion.12 = bf16[4,16,256]{2,1,0:T(8,128)(2,1)S(1)} fusion(f32[4,256,768]{2,1,0:T(8,128)} %fusion.20, f32[4,256,768]{2,1,0:T(8,128)} %copy-done.46, f32[4,256]{1,0:T(4,128)S(1)} %get-tuple-element.236, pred[256,768]{1,0:T(8,128)(4,1)} %copy-done.27, bf16[256,4,16]{0,2,1:T(8,128)(2,1)} %bitcast.162), kind=kOutput, calls=%fused_computation.35 | convolution fusion | flops 36996864 | bytes 6557696 | tf_op jit(solution)/shard_map/while/body/eval_jaxpr/ogw,wox->gox/dot_general | solution.py:213
  327.6 2.9 fusion.74
  330.5 4.7 convolution_bitcast_fusion.4
  337.6 1.9 multiply_reduce_fusion.8
  342.4 4.2 convolution_bitcast_fusion
  347.6 5.4 fusion.15
  353.1 9.3 %fusion.27 = f32[1792,2,1024]{2,0,1:T(8,128)} fusion(bf16[256,1,1024]{2,0,1:T(8,128)(2,1)} %copy-done.23, bf16[256,1,1024]{2,0,1:T(8,128)(2,1)} %copy-done.22, f32[256,1792]{1,0:T(8,128)} %copy-done.1, f32[1792]{0:T(1024)S(1)} %get-tuple-element.184, f32[256]{0:T(256)S(1)} %add_rsqrt_fusion), kind=kOutput, calls=%fused_computation.71 | convolution fusion | flops 1882521600 | bytes 17571840 | tf_op jit(solution)/shard_map/td,tsf->dsf/dot_general | solution.py:170
  362.4 8.5 %copy.109 = bf16[1792,2,1024]{2,0,1:T(8,128)(2,1)} copy(bf16[1792,2,1024]{2,1,0:T(2,128)(2,1)} %param.32) | data formatting | bytes 14680064 | tf_op args[8]
  371.9 2.0 copy.146
  373.9 2.2 constant_dynamic-slice_fusion
  376.1 2.0 copy.147
  379.2 8.0 %reduce-scatter.17.cloned.1.call-done = f32[1024,224]{0,1:T(8,128)} async-done(((f32[1024,1792]{0,1:T(8,128)}), f32[1024,224]{0,1:T(8,128)}) %reduce-scatter.17.cloned.1.call-update) | async-done | bytes 917520 | tf_op jit(solution)/shard_map/reduce_scatter | solution.py:280
  387.3 3.8 multiply_add_fusion.2
  392.0 34.3 %reduce-scatter.21.cloned.1.call-done = f32[224,128]{1,0:T(8,128)} async-done(((f32[1792,128]{1,0:T(8,128)}), f32[224,128]{1,0:T(8,128)}) %reduce-scatter.21.cloned.1.call-update) | async-done | bytes 114704
  429.8 76.9 %all-reduce.18.cloned.1.call-done = f32[256,1792]{1,0:T(8,128)} async-done(((f32[256,1792]{1,0:T(8,128)}), f32[256,1792]{1,0:T(8,128)}) %all-reduce.18.cloned.1.call-update) | async-done | bytes 1835024 | tf_op jit(solution)/shard_map/psum | solution.py:266
  506.8 2.4 multiply_reduce_fusion.2
  509.2 2.9 dynamic-slice_add_fusion
  513.9 2.1 copy.125
  516.1 23.5 %all-reduce.12 = (f32[2,448]{1,0:T(2,128)S(1)}, f32[4,448]{1,0:T(4,128)S(1)}) all-reduce(f32[2,448]{1,0:T(2,128)S(1)} %pad_maximum_fusion.8, f32[4,448]{1,0:T(4,128)S(1)} %pad_maximum_fusion.7), channel_id=1, replica_groups=mesh['dp'=8,'tensor'=4] {'dp'}, use_global_device_ids=true, to_apply=%region_12.13 | all-reduce | flops 2688 | bytes 21504 | tf_op jit(solution)/shard_map/psum | solution.py:274
  540.9 17.0 %reduce-scatter.23.cloned.1.call-done = f32[224,448]{1,0:T(8,128)} async-done(((f32[1792,448]{1,0:T(8,128)}), f32[224,448]{1,0:T(8,128)}) %reduce-scatter.23.cloned.1.call-update) | async-done | bytes 401424
  557.9 2.0 copy.143
  559.9 2.7 multiply_add_fusion.5
  562.6 65.7 %reduce-scatter.13.cloned.1.call-done = f32[224,2,448]{2,0,1:T(8,128)} async-done(((f32[1792,2,448]{2,0,1:T(8,128)}), f32[224,2,448]{2,0,1:T(8,128)}) %reduce-scatter.13.cloned.1.call-update) | async-done | bytes 802832 | tf_op jit(solution)/shard_map/reduce_scatter | solution.py:277
  628.2 2.5 multiply_add_fusion.3
  637.2 96.9 %reduce-scatter.15.cloned.1.call-done = f32[224,2,1024]{2,0,1:T(8,128)} async-done(((f32[1792,2,1024]{2,0,1:T(8,128)}), f32[224,2,1024]{2,0,1:T(8,128)}) %reduce-scatter.15.cloned.1.call-update) | async-done | bytes 1835024 | tf_op jit(solution)/shard_map/reduce_scatter | solution.py:278
  734.1 4.6 multiply_add_fusion
  738.8 2.6 copy.129
  741.4 2.6 copy.131
  744.0 2.6 copy.133
  746.7 2.6 copy.127
  (165 shorter events, 39.5 us)
Async XLA Ops:
  7.2 40.2 %copy-start = (bf16[1792,2,448]{0,2,1:T(8,128)(2,1)S(1)}, bf16[1792,2,448]{0,2,1:T(8,128)(2,1)}, u32[]{:S(2)}) copy-start(bf16[1792,2,448]{0,2,1:T(8,128)(2,1)} %param.29) | copy-start | bytes 9633796
  7.2 26.6 %copy-start.35 = (bf16[2,448]{1,0:T(2,128)(2,1)S(1)}, bf16[2,448]{1,0:T(2,128)(2,1)}, u32[]{:S(2)}) copy-start(bf16[2,448]{1,0:T(2,128)(2,1)} %param.27) | copy-start | bytes 5380
  7.2 136.6 %all-reduce.16.cloned.1.call-start = ((), (), s32[]{:S(2)}) async-start(), calls=%async_computation.6 | async-start | bytes 3670016 | tf_op jit(solution)/shard_map/psum | solution.py:146
  8.2 44.3 %copy-start.40 = (pred[256]{0:T(512)(128)(4,1)}, pred[256]{0:T(512)(128)(4,1)S(1)}, u32[]{:S(2)}) copy-start(pred[256]{0:T(512)(128)(4,1)S(1)} %get-tuple-element.233) | copy-start | bytes 772
  8.2 44.4 %copy-start.41 = (pred[256]{0:T(512)(128)(4,1)}, pred[256]{0:T(512)(128)(4,1)S(1)}, u32[]{:S(2)}) copy-start(pred[256]{0:T(512)(128)(4,1)S(1)} %get-tuple-element.234) | copy-start | bytes 772
  8.3 44.4 %copy-start.42 = (pred[256]{0:T(512)(128)(4,1)}, pred[256]{0:T(512)(128)(4,1)S(1)}, u32[]{:S(2)}) copy-start(pred[256]{0:T(512)(128)(4,1)S(1)} %get-tuple-element.235) | copy-start | bytes 772
  47.4 3.4 copy-start.29
  47.4 3.4 copy-start.31
  47.4 3.4 copy-start.3
  47.4 3.4 copy-start.20
  49.9 4.7 copy-start.17
  50.8 1.9 copy-start.8
  51.6 1.8 copy-start.27
  52.6 2.0 copy-start.46
  53.4 2.0 copy-start.11
  57.3 233.9 %all-gather.4.cloned.1.call-start = ((), (), s32[]{:S(2)}) async-start(), calls=%async_computation.11 | async-start | bytes 9175040 | tf_op jit(solution)/shard_map/all_gather | solution.py:174
  143.8 11.9 %slice-start = ((s8[7340032]{0:T(1024)(128)(4,1)}), s8[4194304]{0:T(1024)(128)(4,1)S(1)}, s32[]{:S(2)}) async-start(s8[7340032]{0:T(1024)(128)(4,1)} %bitcast.137), calls=%async_computation.15 | async-start | bytes 8388608
  146.0 6.4 copy-start.1
  146.1 6.4 copy-start.5
  146.1 6.4 copy-start.28
  146.1 9.6 %slice-start.1 = ((s8[7340032]{0:T(1024)(128)(4,1)}), s8[3145728]{0:T(1024)(128)(4,1)S(1)}, s32[]{:S(2)}) async-start(s8[7340032]{0:T(1024)(128)(4,1)} %bitcast.137), calls=%async_computation.16 | async-start | bytes 6291456
  159.6 218.5 %reduce-scatter.19.cloned.1.call-start = ((), (), s32[]{:S(2)}) async-start(), calls=%async_computation.12 | async-start | bytes 1146880
  164.3 222.9 %reduce-scatter.17.cloned.1.call-start = ((), (), s32[]{:S(2)}) async-start(), calls=%async_computation.10 | async-start | bytes 8257536 | tf_op jit(solution)/shard_map/reduce_scatter | solution.py:280
  170.2 256.1 %reduce-scatter.21.cloned.1.call-start = ((), (), s32[]{:S(2)}) async-start(), calls=%async_computation.13 | async-start | bytes 1032192
  296.2 3.4 copy-start.2
  296.2 3.4 copy-start.4
  299.5 1.9 copy-start.12
  299.5 1.9 copy-start.18
  299.5 2.0 copy-start.25
  301.6 2.1 copy-start.16
  335.3 171.5 %all-reduce.18.cloned.1.call-start = ((), (), s32[]{:S(2)}) async-start(), calls=%async_computation.7 | async-start | bytes 3670016 | tf_op jit(solution)/shard_map/psum | solution.py:266
  335.3 2.3 copy-start.9
  336.8 2.8 copy-start.19
  342.4 215.5 %reduce-scatter.23.cloned.1.call-start = ((), (), s32[]{:S(2)}) async-start(), calls=%async_computation.14 | async-start | bytes 4128768
  346.7 281.6 %reduce-scatter.13.cloned.1.call-start = ((), (), s32[]{:S(2)}) async-start(), calls=%async_computation.8 | async-start | bytes 8257536 | tf_op jit(solution)/shard_map/reduce_scatter | solution.py:277
  353.0 381.1 %reduce-scatter.15.cloned.1.call-start = ((), (), s32[]{:S(2)}) async-start(), calls=%async_computation.9 | async-start | bytes 16515072 | tf_op jit(solution)/shard_map/reduce_scatter | solution.py:278
  379.2 12.8 %copy-start.37 = (f32[448]{0:T(512)S(1)}, f32[448]{0:T(512)}, u32[]{:S(2)}) copy-start(f32[448]{0:T(512)} %get-tuple-element.181) | copy-start | bytes 5380
  379.2 12.8 %copy-start.38 = (f32[448]{0:T(512)S(1)}, f32[448]{0:T(512)}, u32[]{:S(2)}) copy-start(f32[448]{0:T(512)} %get-tuple-element.182) | copy-start | bytes 5380
  379.2 12.7 %copy-start.39 = (f32[448]{0:T(512)S(1)}, f32[448]{0:T(512)}, u32[]{:S(2)}) copy-start(f32[448]{0:T(512)} %get-tuple-element.183) | copy-start | bytes 5380
  509.1 30.5 %copy-start.36 = (bf16[2,448]{1,0:T(2,128)(2,1)S(1)}, bf16[2,448]{1,0:T(2,128)(2,1)}, u32[]{:S(2)}) copy-start(bf16[2,448]{1,0:T(2,128)(2,1)} %param.27) | copy-start | bytes 5380
  509.1 30.5 %copy-start.43 = (f32[2,448]{1,0:T(2,128)S(1)}, f32[2,448]{1,0:T(2,128)}, u32[]{:S(2)}) copy-start(f32[2,448]{1,0:T(2,128)} %param.41) | copy-start | bytes 10756
  509.2 30.5 %copy-start.44 = (f32[2,448]{1,0:T(2,128)S(1)}, f32[2,448]{1,0:T(2,128)}, u32[]{:S(2)}) copy-start(f32[2,448]{1,0:T(2,128)} %param.34) | copy-start | bytes 10756
  509.2 31.1 %copy-start.32 = (f32[4,448]{1,0:T(4,128)S(1)}, f32[4,448]{1,0:T(4,128)}, u32[]{:S(2)}) copy-start(f32[4,448]{1,0:T(4,128)} %param.44) | copy-start | bytes 21508
  509.2 31.1 %copy-start.33 = (f32[4,448]{1,0:T(4,128)S(1)}, f32[4,448]{1,0:T(4,128)}, u32[]{:S(2)}) copy-start(f32[4,448]{1,0:T(4,128)} %param.37) | copy-start | bytes 21508
  539.6 91.1 %copy-start.34 = (f32[4,448]{1,0:T(4,128)}, f32[4,448]{1,0:T(4,128)S(1)}, u32[]{:S(2)}) copy-start(f32[4,448]{1,0:T(4,128)S(1)} %get-tuple-element.187) | copy-start | bytes 21508
  539.6 91.1 %copy-start.45 = (f32[2,448]{1,0:T(2,128)}, f32[2,448]{1,0:T(2,128)S(1)}, u32[]{:S(2)}) copy-start(f32[2,448]{1,0:T(2,128)S(1)} %get-tuple-element.186) | copy-start | bytes 10756
  632.3 3.3 copy-start.10
  744.0 2.6 copy-start.7
  (10 other events, 10.4 us)
Sparse Core Ops, SparseCore 0:
  57.4 86.3 all-reduce.15
  159.7 131.4 all-gather.3
  294.1 23.3 reduce-scatter.18
  321.3 65.8 reduce-scatter.16
  390.9 35.3 reduce-scatter.20
  429.1 77.6 all-reduce.17
  510.2 47.6 reduce-scatter.22
  561.3 66.8 reduce-scatter.12
  631.7 102.3 reduce-scatter.14
